TPU v7x, 32 devices: a whole 2x2x4 slice. The times are simulated.
32 devices in a mesh: pair: 8 (over y, x, core), grp: 4 (over z).
Axes of the slice: x: 2, y: 2, z: 4, core: 2. Of those that a mesh axis runs over, the one named last changes fastest.
Arguments:
- sector_rows: int32 [4], replicated, may hold values from 1 to 256, 768 in all
- wavefunction: bfloat16 [4, 256, 512], P('grp'), may hold values from -6 to 6
- left_ops: bfloat16 [64, 4, 256, 256], P(('pair', 'grp')), may hold values from -0.375 to 0.375
- right_diag: bfloat16 [64, 4, 512], P('pair', 'grp'), may hold values from -0.0078125 to 0.0078125
Outputs:
- slab: float32 [64, 64], P(('pair', 'grp'))
Inputs may be any that keep to these rules, and one draw needn't show every extreme that they name: `sector_rows`: each entry counts the live leading rows of one sector block; at least one sector has 256.
All inputs are finite; a program needn't handle non-finite values.
Results may differ from a plain program's by a relative error of at most 0.0029.
Values may be sent and summed in bfloat16 or wider, within the bound.
No kernel may reach another device: no remote copies, remote signals or barrier semaphores. Data moves between devices by JAX's collectives and lax.ppermute only.
A program may use at most 64 MiB of HBM per device.

v0:
```python
import jax
import jax.numpy as jnp
from jax import lax
from jax.sharding import PartitionSpec as P


def live_states(sector_rows, wavefunction):
    row_index = lax.broadcasted_iota(jnp.int32, wavefunction.shape, 1)
    return jnp.where(
        row_index < sector_rows[:, None, None], wavefunction, jnp.zeros_like(wavefunction)
    )


def local(sector_rows, wavefunction, left_ops, right_diag):
    owned = wavefunction.shape[0]
    first = lax.axis_index("grp") * owned
    right_local = lax.all_gather(right_diag, "pair", axis=0, tiled=True)
    own_rows = lax.dynamic_slice_in_dim(sector_rows, first, owned, 0)
    live = live_states(own_rows, wavefunction)
    blocks = lax.all_to_all(left_ops, "grp", split_axis=1, concat_axis=0, tiled=True)

    def per_pair(block):
        image = jnp.einsum("sab,sbc->sac", block, live, preferred_element_type=jnp.float32)
        return jnp.sum(live.astype(jnp.float32) * image, axis=1)

    weights = lax.map(per_pair, blocks).astype(jnp.bfloat16)
    group_pairs = weights.shape[0]
    flat = weights.reshape(group_pairs, -1)
    diag_flat = right_local.reshape(right_local.shape[0], -1)
    partial_slab = lax.dot_general(
        flat, diag_flat, (((1,), (1,)), ((), ())), preferred_element_type=jnp.float32
    )
    result = lax.psum_scatter(partial_slab, "grp", scatter_dimension=0, tiled=True)
    return result


def solution(mesh):
    in_specs = (
        P(),
        P("grp", None, None),
        P(("pair", "grp"), None, None, None),
        P("pair", "grp", None),
    )
    out_specs = P(("pair", "grp"), None)
    return jax.shard_map(local, mesh=mesh, in_specs=in_specs, out_specs=out_specs, check_vma=False)
```

profile of v0, /device:TPU:0, one launch (start us, length us, event | category | flops | bytes accessed | tf_op | source)
XLA Modules:
  0.0 47.5 jit_solution(5526043052721479483)
XLA Ops:
  0.0 2.3 %copy.8 = bf16[2,4,256,256]{3,2,0,1:T(8,128)(2,1)} copy(bf16[2,4,256,256]{3,2,1,0:T(8,128)(2,1)} %param.8) | data formatting | bytes 2097152 | tf_op args[2]
  2.3 0.0 copy-start.3
  2.3 0.0 copy-start
  2.3 6.5 %all-to-all-start = ((bf16[2,4,256,256]{3,2,0,1:T(8,128)(2,1)}), bf16[2,4,256,256]{3,2,0,1:T(8,128)(2,1)S(1)}, u32[]{:S(2)}, u32[]{:S(2)}) async-start(bf16[2,4,256,256]{3,2,0,1:T(8,128)(2,1)} %copy.8), calls=%async_computation | async-start | bytes 2097152 | tf_op jit(solution)/shard_map/all_to_all | solution.py:20
  8.8 0.0 copy-start.2
  8.8 0.7 %copy-done.2 = s32[4]{0:T(128)S(1)} copy-done((s32[4]{0:T(128)S(1)}, s32[4]{0:T(128)}, u32[]{:S(2)}) %copy-start.2) | copy-done | bytes 40
  9.4 0.6 %dynamic_slice.7 = s32[1]{0:T(128)} dynamic-slice(s32[4]{0:T(128)S(1)} %copy-done.2, s32[]{:T(128)S(6)} %select_n.7), dynamic_slice_sizes={1} | dynamic-slice | bytes 12 | tf_op jit(solution)/shard_map/dynamic_slice | solution.py:18
  10.0 0.0 copy-start.1
  10.0 0.0 copy-done.3
  10.0 0.6 %dynamic-slice = u32[1]{0:T(128)} dynamic-slice(u32[32]{0:T(128)S(1)} %copy-done.3, u32[]{:T(128)S(6)} %add.10), dynamic_slice_sizes={1} | dynamic-slice | bytes 12
  11.3 0.0 copy-done.1
  11.3 9.3 %all_gather.3 = bf16[64,1,512]{2,0,1:T(8,128)(2,1)S(1)} all-gather(bf16[8,1,512]{2,0,1:T(8,128)(2,1)S(1)} %copy-done.1), channel_id=1, replica_groups=mesh['pair'=8,'grp'=4] {'pair'}, dimensions={0}, use_global_device_ids=true | all-gather | bytes 73728 | tf_op jit(solution)/shard_map/all_gather | solution.py:17
  20.6 0.0 copy-done
  20.6 0.7 %fusion.5 = bf16[1,256,512]{2,1,0:T(8,128)(2,1)S(1)} fusion(bf16[1,256,512]{2,1,0:T(8,128)(2,1)S(1)} %copy-done, s32[]{:T(128)} %bitcast.3), kind=kLoop, calls=%fused_computation.7 | loop fusion | flops 262144 | bytes 524292 | tf_op jit(solution)/shard_map/jit(_where)/select_n | solution.py:9
  21.3 13.2 %all-to-all-done = bf16[2,4,256,256]{3,2,0,1:T(8,128)(2,1)S(1)} async-done(((bf16[2,4,256,256]{3,2,0,1:T(8,128)(2,1)}), bf16[2,4,256,256]{3,2,0,1:T(8,128)(2,1)S(1)}, u32[]{:S(2)}, u32[]{:S(2)}) %all-to-all-start) | async-done | bytes 1048608 | tf_op jit(solution)/shard_map/all_to_all | solution.py:20
  34.5 2.5 %while.10 = (s32[]{:T(128)}, bf16[8,1,512]{2,0,1:T(8,128)(2,1)S(1)}, bf16[1,256,512]{2,1,0:T(8,128)(2,1)S(1)}, bf16[8,1,256,256]{3,2,1,0:T(8,128)(2,1)S(1)}, s32[]{:T(128)}, /*index=5*/s32[]{:T(128)}) while((s32[]{:T(128)}, bf16[8,1,512]{2,0,1:T(8,128)(2,1)S(1)}, bf16[1,256,512]{2,1,0:T(8,128)(2,1)S(1)}, ...), condition=%wide.region_2.3_spmd, body=%wide.region_0.2_spmd.sunk | while | flops 67501568 | bytes 661581 | solution.py:26
  34.5 0.2 fusion.15
  34.8 0.2 fusion.15
  35.1 0.2 fusion.15
  35.4 0.2 fusion.15
  35.7 0.2 fusion.15
  36.0 0.2 fusion.15
  36.3 0.2 fusion.15
  36.7 0.2 fusion.15
  37.0 0.1 fusion.6
  37.1 9.8 %all-reduce = f32[8,64]{1,0:T(8,128)S(1)} all-reduce(f32[8,64]{1,0:T(8,128)S(1)} %fusion.6), channel_id=2, replica_groups=mesh['pair'=8,'grp'=4] {'grp'}, use_global_device_ids=true, to_apply=%region_3.4.clone | all-reduce | flops 512 | bytes 4096
  46.9 0.6 %constant_dynamic-slice_fusion = f32[2,64]{1,0:T(2,128)} fusion(f32[8,64]{1,0:T(8,128)S(1)} %all-reduce, u32[]{:T(128)S(6)} %multiply.1), kind=kLoop, calls=%fused_computation.12 | loop fusion | bytes 1028
  (9 shorter events, 0.3 us)
Async XLA Ops:
  2.3 7.8 %copy-start.3 = (u32[32]{0:T(128)S(1)}, u32[32]{0:T(128)}, u32[]{:S(2)}) copy-start(u32[32]{0:T(128)} %constant.28) | copy-start | bytes 388
  2.3 18.3 %copy-start = (bf16[1,256,512]{2,1,0:T(8,128)(2,1)S(1)}, bf16[1,256,512]{2,1,0:T(8,128)(2,1)}, u32[]{:S(2)}) copy-start(bf16[1,256,512]{2,1,0:T(8,128)(2,1)} %param.7) | copy-start | bytes 786436
  2.3 32.2 %all-to-all-start = ((bf16[2,4,256,256]{3,2,0,1:T(8,128)(2,1)}), bf16[2,4,256,256]{3,2,0,1:T(8,128)(2,1)S(1)}, u32[]{:S(2)}, u32[]{:S(2)}) async-start(bf16[2,4,256,256]{3,2,0,1:T(8,128)(2,1)} %copy.8), calls=%async_computation | async-start | bytes 2097152 | tf_op jit(solution)/shard_map/all_to_all | solution.py:20
  8.8 0.7 %copy-start.2 = (s32[4]{0:T(128)S(1)}, s32[4]{0:T(128)}, u32[]{:S(2)}) copy-start(s32[4]{0:T(128)} %param.6) | copy-start | bytes 52
  10.0 1.3 %copy-start.1 = (bf16[8,1,512]{2,0,1:T(8,128)(2,1)S(1)}, bf16[8,1,512]{2,0,1:T(8,128)(2,1)}, u32[]{:S(2)}) copy-start(bf16[8,1,512]{2,0,1:T(8,128)(2,1)} %param.9) | copy-start | bytes 24580
where the time goes:
time: 47.7 us; the launch traced here: 47.5 us
  blocking collectives  19.1 us (40%)
  waiting for transfers between devices  13.2 us (28%)
  starting transfers between devices  6.48 us (14%)
  local copies, waits for them, and re-layouts  5.1 us (11%)
  matrix products  2.07 us (4%)
  other arithmetic  0.7 us (1%)
  between operations  0.67 us (1%)
    all_to_all x1, waiting for transfers between devices, local(): lax.all_to_all(left_ops, 'grp', split_axis=1, concat_axis=0, tiled=True)  13.2 us
    unnamed x1, blocking collectives  9.81 us
    all_gather x1, blocking collectives, local(): right_local = lax.all_gather(right_diag, 'pair', axis=0, tiled=True)  9.26 us
    all_to_all x1, starting transfers between devices, local(): lax.all_to_all(left_ops, 'grp', split_axis=1, concat_axis=0, tiled=True)  6.48 us
    unnamed x11, local copies, waits for them, and re-layouts  4.15 us
    dot_general x8, matrix products, per_pair(): jnp.einsum('sab,sbc->sac', block, live, preferred_element_type=jnp.float32)  1.95 us
  transfers between devices with their start and end apart: 1, of which 1 were waited for; matrix products, arithmetic and copies ran while one was open for 4% of the time, Pallas kernels for 0%

commit v1 on v0

--- a/solution.py
+++ b/solution.py
@@ -17,7 +17,21 @@
     right_local = lax.all_gather(right_diag, "pair", axis=0, tiled=True)
     own_rows = lax.dynamic_slice_in_dim(sector_rows, first, owned, 0)
     live = live_states(own_rows, wavefunction)
-    blocks = lax.all_to_all(left_ops, "grp", split_axis=1, concat_axis=0, tiled=True)
+    h_now, back = (lax.axis_size("grp"), lax.axis_index("grp"))
+    local_now = left_ops.shape[1] // h_now
+    taken_in = list(left_ops.shape)
+    taken_in[1] = local_now
+    local_next = taken_in[0]
+    taken_in[0] = local_next * h_now
+    blocks = jnp.zeros(taken_in, left_ops.dtype)
+    for j in range(h_now):
+        w1 = lax.dynamic_slice_in_dim(left_ops, (back ^ j) * local_now, local_now, axis=1)
+        if j:
+            fields = []
+            for ix in range(h_now):
+                fields.append((ix, ix ^ j))
+            w1 = lax.ppermute(w1, "grp", perm=fields)
+        blocks = lax.dynamic_update_slice_in_dim(blocks, w1, (back ^ j) * local_next, axis=0)
 
     def per_pair(block):
         image = jnp.einsum("sab,sbc->sac", block, live, preferred_element_type=jnp.float32)

time: 47.7 us -> 42.3 us (0.89)
  waiting for transfers between devices: 13.2 us -> 6.02 us
  blocking collectives: 19.1 us -> 22.6 us
  local copies, waits for them, and re-layouts: 5.1 us -> 4.05 us
  starting transfers between devices: 6.48 us -> 5.71 us
    all_to_all x1 -> x0, waiting for transfers between devices: 13.2 us -> none  [local(): lax.all_to_all(left_ops, 'grp', split_axis=1, concat_axis=0, tiled=True)]
    all_to_all x1 -> x0, starting transfers between devices: 6.48 us -> none  [local(): lax.all_to_all(left_ops, 'grp', split_axis=1, concat_axis=0, tiled=True)]
    ppermute x0 -> x3, waiting for transfers between devices: none -> 6.02 us  [local(): w1 = lax.ppermute(w1, 'grp', perm=fields)]
    ppermute x0 -> x3, starting transfers between devices: none -> 5.71 us  [local(): w1 = lax.ppermute(w1, 'grp', perm=fields)]
    unnamed x1, blocking collectives: 9.81 us -> 13.1 us
    unnamed x11 -> x12, local copies, waits for them, and re-layouts: 4.15 us -> 2.92 us
  transfers between devices with their start and end apart: 1 -> 3, of which waited for: 1 -> 1; matrix products, arithmetic and copies ran while one was open for 4% -> 5% of each run, Pallas kernels for 0% -> 0%
where the time goes in v1:
time: 42.3 us; the launch traced here: 42.1 us
  blocking collectives  22.6 us (53%)
  waiting for transfers between devices  6.02 us (14%)
  starting transfers between devices  5.71 us (13%)
  local copies, waits for them, and re-layouts  4.05 us (10%)
  matrix products  2.08 us (5%)
  between operations  0.75 us (2%)
  other arithmetic  0.71 us (2%)
    unnamed x1, blocking collectives  13.1 us
    all_gather x1, blocking collectives, local(): right_local = lax.all_gather(right_diag, 'pair', axis=0, tiled=True)  9.48 us
    ppermute x3, waiting for transfers between devices, local(): w1 = lax.ppermute(w1, 'grp', perm=fields)  6.02 us
    ppermute x3, starting transfers between devices, local(): w1 = lax.ppermute(w1, 'grp', perm=fields)  5.71 us
    unnamed x12, local copies, waits for them, and re-layouts  2.92 us
    dot_general x8, matrix products, per_pair(): jnp.einsum('sab,sbc->sac', block, live, preferred_element_type=jnp.float32)  1.95 us
  transfers between devices with their start and end apart: 3, of which 1 were waited for; matrix products, arithmetic and copies ran while one was open for 5% of the time, Pallas kernels for 0%

profile of v1, /device:TPU:0, one launch (start us, length us, event | category | flops | bytes accessed | tf_op | source)
XLA Modules:
  0.0 42.1 jit_solution(16885321399417180998)
XLA Ops:
  0.0 0.0 copy-start
  0.0 0.1 broadcast_in_dim.16
  0.1 1.1 %copy-done = bf16[2,4,256,256]{3,2,1,0:T(8,128)(2,1)S(1)} copy-done((bf16[2,4,256,256]{3,2,1,0:T(8,128)(2,1)S(1)}, bf16[2,4,256,256]{3,2,1,0:T(8,128)(2,1)}, u32[]{:S(2)}) %copy-start) | copy-done | bytes 1048600
  1.2 0.0 copy-start.1
  1.2 0.1 constant_dynamic-slice_fusion
  1.3 3.1 %collective-permute-start = (bf16[2,1,256,256]{3,2,1,0:T(8,128)(2,1)S(1)}, bf16[2,1,256,256]{3,2,1,0:T(8,128)(2,1)S(1)}, u32[]{:S(2)}, u32[]{:S(2)}) collective-permute-start(bf16[2,1,256,256]{3,2,1,0:T(8,128)(2,1)S(1)} %get-tuple-element.37), channel_id=1, source_target_pairs={{0,1},{1,0},{2,3},{3,2},{4,5},{5,4},{6,7},{7,6},{8,9},{9,8},{10,11... | collective-permute-start | bytes 786440 | tf_op jit(solution)/shard_map/ppermute | solution.py:33
  4.4 0.0 copy-start.3
  4.4 2.6 %collective-permute-start.1 = (bf16[2,1,256,256]{3,2,1,0:T(8,128)(2,1)S(1)}, bf16[2,1,256,256]{3,2,1,0:T(8,128)(2,1)S(1)}, u32[]{:S(2)}, u32[]{:S(2)}) collective-permute-start(bf16[2,1,256,256]{3,2,1,0:T(8,128)(2,1)S(1)} %get-tuple-element.39), channel_id=1, source_target_pairs={{0,2},{1,3},{2,0},{3,1},{4,6},{5,7},{6,4},{7,5},{8,10},{9,11},{10,... | collective-permute-start | bytes 786440 | tf_op jit(solution)/shard_map/ppermute | solution.py:33
  7.0 0.0 collective-permute-start.2
  7.0 0.0 copy-done.3
  7.0 0.6 %dynamic_slice.19 = s32[1]{0:T(128)} dynamic-slice(s32[4]{0:T(128)S(1)} %copy-done.3, s32[]{:T(128)S(6)} %select_n.29), dynamic_slice_sizes={1} | dynamic-slice | bytes 12 | tf_op jit(solution)/shard_map/dynamic_slice | solution.py:18
  7.6 0.0 copy-done.1
  7.6 0.7 %fusion.5 = bf16[1,256,512]{2,1,0:T(8,128)(2,1)S(1)} fusion(bf16[1,256,512]{2,1,0:T(8,128)(2,1)S(1)} %copy-done.1, s32[]{:T(128)} %bitcast.3), kind=kLoop, calls=%fused_computation.7 | loop fusion | flops 262144 | bytes 524292 | tf_op jit(solution)/shard_map/jit(_where)/select_n | solution.py:9
  8.3 0.0 copy-start.4
  8.4 0.0 copy-start.2
  8.4 0.6 %copy-done.4 = u32[32]{0:T(128)S(1)} copy-done((u32[32]{0:T(128)S(1)}, u32[32]{0:T(128)}, u32[]{:S(2)}) %copy-start.4) | copy-done | bytes 152
  9.0 0.6 %dynamic-slice = u32[1]{0:T(128)} dynamic-slice(u32[32]{0:T(128)S(1)} %copy-done.4, u32[]{:T(128)S(6)} %add.39), dynamic_slice_sizes={1} | dynamic-slice | bytes 12
  10.2 0.0 copy-done.2
  10.2 9.5 %all_gather.3 = bf16[64,1,512]{2,0,1:T(8,128)(2,1)S(1)} all-gather(bf16[8,1,512]{2,0,1:T(8,128)(2,1)S(1)} %copy-done.2), channel_id=1, replica_groups=mesh['pair'=8,'grp'=4] {'pair'}, dimensions={0}, use_global_device_ids=true | all-gather | bytes 73728 | tf_op jit(solution)/shard_map/all_gather | solution.py:17
  19.7 0.0 collective-permute-done
  19.7 6.0 %collective-permute-done.1 = bf16[2,1,256,256]{3,2,1,0:T(8,128)(2,1)S(1)} collective-permute-done((bf16[2,1,256,256]{3,2,1,0:T(8,128)(2,1)S(1)}, bf16[2,1,256,256]{3,2,1,0:T(8,128)(2,1)S(1)}, u32[]{:S(2)}, u32[]{:S(2)}) %collective-permute-start.1) | collective-permute-done | bytes 262176 | tf_op jit(solution)/shard_map/ppermute | solution.py:33
  25.8 0.0 collective-permute-done.2
  25.8 2.5 %while.10 = (s32[]{:T(128)}, bf16[8,1,512]{2,0,1:T(8,128)(2,1)S(1)}, bf16[1,256,512]{2,1,0:T(8,128)(2,1)S(1)}, bf16[8,1,256,256]{3,2,1,0:T(8,128)(2,1)S(1)}, s32[]{:T(128)}, /*index=5*/s32[]{:T(128)}) while((s32[]{:T(128)}, bf16[8,1,512]{2,0,1:T(8,128)(2,1)S(1)}, bf16[1,256,512]{2,1,0:T(8,128)(2,1)S(1)}, ...), condition=%wide.region_2.3_spmd, body=%wide.region_0.2_spmd.sunk | while | flops 67501568 | bytes 661581 | solution.py:40
  25.8 0.2 fusion.15
  26.1 0.2 fusion.15
  26.4 0.2 fusion.15
  26.7 0.2 fusion.15
  27.1 0.2 fusion.15
  27.4 0.2 fusion.15
  27.7 0.2 fusion.15
  28.0 0.2 fusion.15
  28.3 0.1 fusion.6
  28.4 13.1 %all-reduce = f32[8,64]{1,0:T(8,128)S(1)} all-reduce(f32[8,64]{1,0:T(8,128)S(1)} %fusion.6), channel_id=2, replica_groups=mesh['pair'=8,'grp'=4] {'grp'}, use_global_device_ids=true, to_apply=%region_3.4.clone | all-reduce | flops 512 | bytes 4096
  41.5 0.6 %constant_dynamic-slice_fusion.3 = f32[2,64]{1,0:T(2,128)} fusion(f32[8,64]{1,0:T(8,128)S(1)} %all-reduce, u32[]{:T(128)S(6)} %multiply.1), kind=kLoop, calls=%fused_computation.19 | loop fusion | bytes 1028
  (12 shorter events, 0.4 us)
Async XLA Ops:
  0.0 1.2 %copy-start = (bf16[2,4,256,256]{3,2,1,0:T(8,128)(2,1)S(1)}, bf16[2,4,256,256]{3,2,1,0:T(8,128)(2,1)}, u32[]{:S(2)}) copy-start(bf16[2,4,256,256]{3,2,1,0:T(8,128)(2,1)} %param.8) | copy-start | bytes 3145732
  1.2 6.4 %copy-start.1 = (bf16[1,256,512]{2,1,0:T(8,128)(2,1)S(1)}, bf16[1,256,512]{2,1,0:T(8,128)(2,1)}, u32[]{:S(2)}) copy-start(bf16[1,256,512]{2,1,0:T(8,128)(2,1)} %param.7) | copy-start | bytes 786436
  1.3 18.4 %collective-permute-start = (bf16[2,1,256,256]{3,2,1,0:T(8,128)(2,1)S(1)}, bf16[2,1,256,256]{3,2,1,0:T(8,128)(2,1)S(1)}, u32[]{:S(2)}, u32[]{:S(2)}) collective-permute-start(bf16[2,1,256,256]{3,2,1,0:T(8,128)(2,1)S(1)} %get-tuple-element.37), channel_id=1, source_target_pairs={{0,1},{1,0},{2,3},{3,2},{4,5},{5,4},{6,7},{7,6},{8,9},{9,8},{10,11... | collective-permute-start | bytes 786440 | tf_op jit(solution)/shard_map/ppermute | solution.py:33
  4.4 2.6 %copy-start.3 = (s32[4]{0:T(128)S(1)}, s32[4]{0:T(128)}, u32[]{:S(2)}) copy-start(s32[4]{0:T(128)} %param.6) | copy-start | bytes 52
  4.4 21.3 %collective-permute-start.1 = (bf16[2,1,256,256]{3,2,1,0:T(8,128)(2,1)S(1)}, bf16[2,1,256,256]{3,2,1,0:T(8,128)(2,1)S(1)}, u32[]{:S(2)}, u32[]{:S(2)}) collective-permute-start(bf16[2,1,256,256]{3,2,1,0:T(8,128)(2,1)S(1)} %get-tuple-element.39), channel_id=1, source_target_pairs={{0,2},{1,3},{2,0},{3,1},{4,6},{5,7},{6,4},{7,5},{8,10},{9,11},{10,... | collective-permute-start | bytes 786440 | tf_op jit(solution)/shard_map/ppermute | solution.py:33
  7.0 18.8 %collective-permute-start.2 = (bf16[2,1,256,256]{3,2,1,0:T(8,128)(2,1)S(1)}, bf16[2,1,256,256]{3,2,1,0:T(8,128)(2,1)S(1)}, u32[]{:S(2)}, u32[]{:S(2)}) collective-permute-start(bf16[2,1,256,256]{3,2,1,0:T(8,128)(2,1)S(1)} %get-tuple-element.36), channel_id=1, source_target_pairs={{0,3},{1,2},{2,1},{3,0},{4,7},{5,6},{6,5},{7,4},{8,11},{9,10},{10,... | collective-permute-start | bytes 786440 | tf_op jit(solution)/shard_map/ppermute | solution.py:33
  8.3 0.7 %copy-start.4 = (u32[32]{0:T(128)S(1)}, u32[32]{0:T(128)}, u32[]{:S(2)}) copy-start(u32[32]{0:T(128)} %constant.37) | copy-start | bytes 388
  8.4 1.8 %copy-start.2 = (bf16[8,1,512]{2,0,1:T(8,128)(2,1)S(1)}, bf16[8,1,512]{2,0,1:T(8,128)(2,1)}, u32[]{:S(2)}) copy-start(bf16[8,1,512]{2,0,1:T(8,128)(2,1)} %param.9) | copy-start | bytes 24580
